TPU v7x, 32 devices: a whole 2x2x4 slice. The times are simulated.
32 devices in a mesh: dp: 8 (over y, x, core), blk: 4 (over z).
Axes of the slice: x: 2, y: 2, z: 4, core: 2. Of those that a mesh axis runs over, the one named last changes fastest.
Arguments:
- tokens: bfloat16 [24, 1024, 1024], P('dp', 'blk'), may hold values from -6 to 6
- cotangent: bfloat16 [24, 1024, 1024], P('dp', 'blk'), may hold values from -6 to 6
- domain_ids: int32 [24, 1024], P('dp', 'blk'), may hold values from 0 to 21
- domain_weight: float32 [22], replicated, may hold values from 0.3 to 3
- frozen_input_weights: bfloat16 [1024, 8192], P('dp'), may hold values from -0.1875 to 0.1875
- bias_in: bfloat16 [8192], replicated, may hold values from -1.25 to 1.25
- frozen_down_weight: bfloat16 [4096, 1024], P('dp'), may hold values from -0.09375 to 0.09375
- bias_ff: bfloat16 [1024], replicated, may hold values from -1.25 to 1.25
- norm_gain: float32 [2, 1024], replicated, may hold values from 0.5 to 1.5
- norm_shift: float32 [2, 1024], replicated, may hold values from -1.25 to 1.25
- adapt_a: float32 [1024, 384], P('dp'), may hold values from -0.1875 to 0.1875
- adapt_a_ff: float32 [4096, 128], P('dp'), may hold values from -0.09375 to 0.09375
- adapt_b: float32 [128, 8192], P(None, 'dp'), may hold values from -0.5 to 0.5
- adapt_b_ff: float32 [128, 1024], P(None, 'dp'), may hold values from -0.5 to 0.5
- mean_a: float32 [1024, 384], P('dp'), may hold values from -192 to 192
- mean_a_ff: float32 [4096, 128], P('dp'), may hold values from -192 to 192
- mean_b: float32 [128, 8192], P(None, 'dp'), may hold values from -192 to 192
- mean_b_ff: float32 [128, 1024], P(None, 'dp'), may hold values from -192 to 192
- square_a: float32 [1024, 384], P('dp'), may hold values from 100 to 100000
- square_a_ff: float32 [4096, 128], P('dp'), may hold values from 100 to 100000
- square_b: float32 [128, 8192], P(None, 'dp'), may hold values from 100 to 100000
- square_b_ff: float32 [128, 1024], P(None, 'dp'), may hold values from 100 to 100000
- keep_a: int32 [1024, 384], P('dp'), may hold values 0 or 1
- keep_a_ff: int32 [4096, 128], P('dp'), may hold values 0 or 1
- keep_b: int32 [128, 8192], P(None, 'dp'), may hold values 0 or 1
- keep_b_ff: int32 [128, 1024], P(None, 'dp'), may hold values 0 or 1
Outputs:
- mixed: bfloat16 [24, 1024, 1024], P('dp', 'blk')
- grad_tokens: bfloat16 [24, 1024, 1024], P('dp', 'blk')
- grad_gain: float32 [2, 1024], replicated
- grad_shift: float32 [2, 1024], replicated
- grad_a: float32 [1024, 384], P('dp')
- grad_a_ff: float32 [4096, 128], P('dp')
- grad_b: float32 [128, 8192], P(None, 'dp')
- grad_b_ff: float32 [128, 1024], P(None, 'dp')
- new_mean_a: float32 [1024, 384], P('dp')
- new_square_a: float32 [1024, 384], P('dp')
- new_mean_a_ff: float32 [4096, 128], P('dp')
- new_square_a_ff: float32 [4096, 128], P('dp')
- new_mean_b: float32 [128, 8192], P(None, 'dp')
- new_square_b: float32 [128, 8192], P(None, 'dp')
- new_mean_b_ff: float32 [128, 1024], P(None, 'dp')
- new_square_b_ff: float32 [128, 1024], P(None, 'dp')
- folded_input_weights: bfloat16 [1024, 8192], P('dp')
- folded_down_weight: bfloat16 [4096, 1024], P('dp')
All inputs are finite; a program needn't handle non-finite values. No bound on the sum of `keep_a` or of `keep_a_ff` or of `keep_b` or of `keep_b_ff` on one device may be relied on, other than what follows from the above.
Results may differ from a plain program's by a relative error of at most 0.025.
Values may be sent and summed in bfloat16 or wider, within the bound.
A program may use at most 320 MiB of HBM per device.

v0:
```python
import math
import jax
import jax.numpy as jnp
from jax import lax
from jax.sharding import PartitionSpec as P

HEADS = 16
ROTARY = 16
DOMAINS = 22
highest = lax.Precision.HIGHEST
adapter_scale = 0.25
rope_base = 10000.0
norm_eps = 1e-05
masked_score = -1e30
first_fix = 1.0 - (0.9**10) ** 10
second_fix = 1.0 - (0.999**10) ** 10


def matrix_product(left, right):
    return jnp.dot(left, right, preferred_element_type=jnp.float32)


def product_right_transposed(left, right):
    return lax.dot_general(
        left, right, (((1,), (1,)), ((), ())), preferred_element_type=jnp.float32
    )


def product_left_transposed(left, right):
    return lax.dot_general(
        left, right, (((0,), (0,)), ((), ())), preferred_element_type=jnp.float32
    )


def precise_product(left, right):
    return jnp.dot(left, right, precision=highest)


def layer_norm(values, gain, shift):
    centre = values - jnp.mean(values, axis=-1, keepdims=True)
    spread = jnp.mean(centre * centre, axis=-1, keepdims=True)
    return centre * lax.rsqrt(spread + norm_eps) * gain + shift


def exact_gelu(values):
    return jax.nn.gelu(values, approximate=False)


def rope_tables(positions, rotary):
    half = rotary // 2
    freqs = rope_base ** (-(jnp.arange(half, dtype=jnp.float32) * 2.0) / rotary)
    angles = positions.astype(jnp.float32)[:, None] * freqs[None, :]
    return (jnp.cos(angles), jnp.sin(angles))


def rotate(values, cosine, sine, rotary):
    half = rotary // 2
    front = values[..., :half]
    back = values[..., half:rotary]
    rest = values[..., rotary:]
    cos_b = cosine[:, None, :]
    sin_b = sine[:, None, :]
    return jnp.concatenate(
        [front * cos_b - back * sin_b, back * cos_b + front * sin_b, rest], axis=-1
    )


def project(input_rows, weight_matrix, bias_vector, down, upper_factor):
    middle_rows = matrix_product(input_rows, down).astype(jnp.bfloat16)
    return (
        matrix_product(input_rows, weight_matrix)
        + bias_vector.astype(jnp.float32)
        + adapter_scale * matrix_product(middle_rows, upper_factor),
        middle_rows,
    )


def project_back(
    output_gradient, input_rows, middle_rows, weight_matrix, bias_vector, down, upper_factor
):
    middle_gradient = (
        adapter_scale * product_right_transposed(output_gradient, upper_factor)
    ).astype(jnp.bfloat16)
    upper_gradient = adapter_scale * product_left_transposed(middle_rows, output_gradient)
    grad_down = product_left_transposed(input_rows, middle_gradient)
    grad_in = product_right_transposed(output_gradient, weight_matrix) + product_right_transposed(
        middle_gradient, down
    )
    return (grad_in, grad_down, upper_gradient)


def split_blocks(full, bias_in, bias_ff, width, rank):
    w_all, w_ff, a_all, a_ff, b_all, b_ff = full
    part_qkv = (w_all[:, : 3 * width], bias_in[: 3 * width], a_all[:, :rank], b_all[:, : 3 * width])
    part_att = (
        w_all[:, 3 * width : 4 * width],
        bias_in[3 * width : 4 * width],
        a_all[:, rank : 2 * rank],
        b_all[:, 3 * width : 4 * width],
    )
    part_up = (
        w_all[:, 4 * width :],
        bias_in[4 * width :],
        a_all[:, 2 * rank :],
        b_all[:, 4 * width :],
    )
    part_ff = (w_ff, bias_ff, a_ff, b_ff)
    return (part_qkv, part_att, part_up, part_ff)


def adam_update(param, grad, mean, square, keep):
    mean_new = 0.9 * mean + 0.1 * grad
    square_new = 0.999 * square + 0.001 * grad * grad
    fresh = param - 0.01 * (mean_new / first_fix) / (jnp.sqrt(square_new / second_fix) + 1e-08)
    kept = keep.astype(jnp.float32)
    return (fresh, mean_new * kept, square_new * kept)


def body(
    tokens,
    cotangent,
    domain_ids,
    domain_weight,
    frozen_input_weights,
    bias_in,
    frozen_down_weight,
    bias_ff,
    norm_gain,
    norm_shift,
    adapt_a,
    adapt_a_ff,
    adapt_b,
    adapt_b_ff,
    mean_a,
    mean_a_ff,
    mean_b,
    mean_b_ff,
    square_a,
    square_a_ff,
    square_b,
    square_b_ff,
    keep_a,
    keep_a_ff,
    keep_b,
    keep_b_ff,
):
    seqs, span, width = tokens.shape
    rows = seqs * span
    rank = adapt_b.shape[0]
    depth = width // HEADS
    att_scale = 1.0 / math.sqrt(depth)
    shards = (
        frozen_input_weights,
        frozen_down_weight,
        adapt_a.astype(jnp.bfloat16),
        adapt_a_ff.astype(jnp.bfloat16),
        adapt_b.astype(jnp.bfloat16),
        adapt_b_ff.astype(jnp.bfloat16),
    )
    whole = (
        lax.all_gather(shards[0], "dp", axis=0, tiled=True),
        lax.all_gather(shards[1], "dp", axis=0, tiled=True),
        lax.all_gather(shards[2], "dp", axis=0, tiled=True),
        lax.all_gather(shards[3], "dp", axis=0, tiled=True),
        lax.all_gather(shards[4], "dp", axis=1, tiled=True),
        lax.all_gather(shards[5], "dp", axis=1, tiled=True),
    )
    part_qkv, part_att, part_up, part_ff = split_blocks(whole, bias_in, bias_ff, width, rank)
    input_rows = tokens.astype(jnp.float32).reshape(rows, width)
    first_f, first_pull = jax.vjp(layer_norm, input_rows, norm_gain[0], norm_shift[0])
    second_f, second_pull = jax.vjp(layer_norm, input_rows, norm_gain[1], norm_shift[1])
    first = first_f.astype(jnp.bfloat16)
    second = second_f.astype(jnp.bfloat16)
    joint, middle_qkv = project(first, *part_qkv)
    joint3 = joint.reshape(seqs, span, 3 * width)
    positions = lax.axis_index("blk") * span + jnp.arange(span, dtype=jnp.int32)
    cosine, sine = rope_tables(positions, ROTARY)

    def turn(query_raw, key_raw):
        return (rotate(query_raw, cosine, sine, ROTARY), rotate(key_raw, cosine, sine, ROTARY))

    (query_r, key_r), rope_pull = jax.vjp(
        turn,
        joint3[..., :width].reshape(seqs, span, HEADS, depth),
        joint3[..., width : 2 * width].reshape(seqs, span, HEADS, depth),
    )
    query_b = query_r.astype(jnp.bfloat16)
    key_local = key_r.astype(jnp.bfloat16)
    value_local = joint3[..., 2 * width :].reshape(seqs, span, HEADS, depth).astype(jnp.bfloat16)
    key_send = key_local.reshape(seqs, span, width)
    value_send = value_local.reshape(seqs, span, width)
    top = jnp.full((seqs, HEADS, span), masked_score, jnp.float32)
    key_piece = lax.all_gather(key_send, "blk", axis=1, tiled=True)
    value_piece = lax.all_gather(value_send, "blk", axis=1, tiled=True)
    count = key_piece.shape[1]
    key_h = key_piece.reshape(seqs, count, HEADS, depth)
    value_h = value_piece.reshape(seqs, count, HEADS, depth)
    scores = (
        jnp.einsum("sqhe,skhe->shqk", query_b, key_h, preferred_element_type=jnp.float32)
        * att_scale
    )
    allowed = positions[:, None] >= jnp.arange(count, dtype=jnp.int32)[None, :]
    scores = jnp.where(allowed, scores, masked_score)
    new_top = jnp.maximum(top, jnp.max(scores, axis=-1))
    weights = jnp.where(allowed, jnp.exp(scores - new_top[..., None]), 0.0)
    total = jnp.sum(weights, axis=-1)
    update = jnp.einsum(
        "shqk,skhe->sqhe", weights.astype(jnp.bfloat16), value_h, preferred_element_type=jnp.float32
    )
    accum = update
    top, total, accum = (new_top, total, accum)
    attended_f = (accum / jnp.transpose(total, (0, 2, 1))[..., None]).reshape(rows, width)
    log_total = top + jnp.log(total)
    attended = attended_f.astype(jnp.bfloat16)
    branch_att, middle_att = project(attended, *part_att)
    up_pre, middle_up = project(second, *part_up)
    hidden_f, gelu_pull = jax.vjp(exact_gelu, up_pre)
    hidden = hidden_f.astype(jnp.bfloat16)
    branch_ff, middle_ff = project(hidden, *part_ff)
    mixed = (input_rows + branch_att + branch_ff).astype(jnp.bfloat16).reshape(seqs, span, width)
    lookup = (domain_ids[..., None] == jnp.arange(DOMAINS, dtype=jnp.int32)).astype(jnp.float32)
    row_weight = jnp.sum(lookup * domain_weight, axis=-1).reshape(rows, 1)
    row_grad = cotangent.astype(jnp.float32).reshape(rows, width) * row_weight
    grad_low = row_grad.astype(jnp.bfloat16)
    grad_hidden, grad_a_ffp, grad_b_ffp = project_back(grad_low, hidden, middle_ff, *part_ff)
    upper_gradient = gelu_pull(grad_hidden)[0].astype(jnp.bfloat16)
    grad_second, grad_a_up, grad_b_up = project_back(upper_gradient, second, middle_up, *part_up)
    grad_att_f, grad_a_att, grad_b_att = project_back(grad_low, attended, middle_att, *part_att)
    grad_att = grad_att_f.astype(jnp.bfloat16)
    grad_heads = grad_att.reshape(seqs, span, HEADS, depth)
    delta = jnp.transpose(
        jnp.sum(
            grad_heads.astype(jnp.float32) * attended_f.reshape(seqs, span, HEADS, depth), axis=-1
        ),
        (0, 2, 1),
    )
    key_piece = lax.all_gather(key_send, "blk", axis=1, tiled=True)
    value_piece = lax.all_gather(value_send, "blk", axis=1, tiled=True)
    count = key_piece.shape[1]
    key_h = key_piece.reshape(seqs, count, HEADS, depth)
    value_h = value_piece.reshape(seqs, count, HEADS, depth)
    scores = (
        jnp.einsum("sqhe,skhe->shqk", query_b, key_h, preferred_element_type=jnp.float32)
        * att_scale
    )
    allowed = positions[:, None] >= jnp.arange(count, dtype=jnp.int32)[None, :]
    weights = jnp.where(allowed, jnp.exp(scores - log_total[..., None]), 0.0)
    grad_w = jnp.einsum("sqhe,skhe->shqk", grad_heads, value_h, preferred_element_type=jnp.float32)
    grad_s = (weights * (grad_w - delta[..., None])).astype(jnp.bfloat16)
    grad_query = (
        jnp.einsum("shqk,skhe->sqhe", grad_s, key_h, preferred_element_type=jnp.float32) * att_scale
    )
    stats_lse, stats_delta = (
        lax.all_gather(log_total.astype(jnp.bfloat16), "blk", axis=2, tiled=True).astype(
            log_total.dtype
        ),
        lax.all_gather(delta.astype(jnp.bfloat16), "blk", axis=2, tiled=True).astype(delta.dtype),
    )
    query_piece = lax.all_gather(query_b.reshape(seqs, span, width), "blk", axis=1, tiled=True)
    grad_piece = lax.all_gather(grad_att.reshape(seqs, span, width), "blk", axis=1, tiled=True)
    count = query_piece.shape[1]
    query_h = query_piece.reshape(seqs, count, HEADS, depth)
    grad_h = grad_piece.reshape(seqs, count, HEADS, depth)
    scores = (
        jnp.einsum("sqhe,skhe->shqk", query_h, key_local, preferred_element_type=jnp.float32)
        * att_scale
    )
    allowed = jnp.arange(count, dtype=jnp.int32)[:, None] >= positions[None, :]
    weights = jnp.where(allowed, jnp.exp(scores - stats_lse[..., None]), 0.0)
    grad_v = jnp.einsum(
        "shqk,sqhe->skhe", weights.astype(jnp.bfloat16), grad_h, preferred_element_type=jnp.float32
    )
    grad_w = jnp.einsum("sqhe,skhe->shqk", grad_h, value_local, preferred_element_type=jnp.float32)
    grad_s = (weights * (grad_w - stats_delta[..., None])).astype(jnp.bfloat16)
    grad_k = (
        jnp.einsum("shqk,sqhe->skhe", grad_s, query_h, preferred_element_type=jnp.float32)
        * att_scale
    )
    grad_query_raw, grad_key_raw = rope_pull((grad_query, grad_k))
    grad_joint = jnp.concatenate(
        [
            grad_query_raw.reshape(rows, width),
            grad_key_raw.reshape(rows, width),
            grad_v.reshape(rows, width),
        ],
        axis=1,
    ).astype(jnp.bfloat16)
    grad_first, grad_a_qkv, grad_b_qkv = project_back(grad_joint, first, middle_qkv, *part_qkv)
    back_one = first_pull(grad_first)
    back_two = second_pull(grad_second)
    grad_tokens = (
        (row_grad + back_one[0] + back_two[0]).astype(jnp.bfloat16).reshape(seqs, span, width)
    )
    gain_part = jnp.stack([back_one[1], back_two[1]])
    shift_part = jnp.stack([back_one[2], back_two[2]])
    grad_a_part = jnp.concatenate([grad_a_qkv, grad_a_att, grad_a_up], axis=1)
    grad_b_part = jnp.concatenate([grad_b_qkv, grad_b_att, grad_b_up], axis=1)
    summed = lax.psum(
        (grad_a_part, grad_a_ffp, grad_b_part, grad_b_ffp, gain_part, shift_part), ("dp", "blk")
    )
    owner = lax.axis_index("dp")
    grad_a = lax.dynamic_slice_in_dim(summed[0], owner * adapt_a.shape[0], adapt_a.shape[0], 0)
    grad_a_ff = lax.dynamic_slice_in_dim(
        summed[1], owner * adapt_a_ff.shape[0], adapt_a_ff.shape[0], 0
    )
    grad_b = lax.dynamic_slice_in_dim(summed[2], owner * adapt_b.shape[1], adapt_b.shape[1], 1)
    grad_b_ff = lax.dynamic_slice_in_dim(
        summed[3], owner * adapt_b_ff.shape[1], adapt_b_ff.shape[1], 1
    )
    grad_gain = summed[4]
    grad_shift = summed[5]
    fresh_a, new_mean_a, new_square_a = adam_update(adapt_a, grad_a, mean_a, square_a, keep_a)
    reset_down_adapter_left, new_mean_a_ff, new_square_a_ff = adam_update(
        adapt_a_ff, grad_a_ff, mean_a_ff, square_a_ff, keep_a_ff
    )
    fresh_b, new_mean_b, new_square_b = adam_update(adapt_b, grad_b, mean_b, square_b, keep_b)
    reset_down_adapter_right, new_mean_b_ff, new_square_b_ff = adam_update(
        adapt_b_ff, grad_b_ff, mean_b_ff, square_b_ff, keep_b_ff
    )
    fresh_b_all, reset_down_right_stacked = (
        lax.all_gather(fresh_b.astype(jnp.bfloat16), "dp", axis=1, tiled=True).astype(
            fresh_b.dtype
        ),
        lax.all_gather(
            reset_down_adapter_right.astype(jnp.bfloat16), "dp", axis=1, tiled=True
        ).astype(reset_down_adapter_right.dtype),
    )
    input_weight_update = jnp.concatenate(
        [
            precise_product(fresh_a[:, :rank], fresh_b_all[:, : 3 * width]),
            precise_product(fresh_a[:, rank : 2 * rank], fresh_b_all[:, 3 * width : 4 * width]),
            precise_product(fresh_a[:, 2 * rank :], fresh_b_all[:, 4 * width :]),
        ],
        axis=1,
    )
    folded_input_weights = (
        frozen_input_weights.astype(jnp.float32) + adapter_scale * input_weight_update
    ).astype(jnp.bfloat16)
    folded_down_weight = (
        frozen_down_weight.astype(jnp.float32)
        + adapter_scale * precise_product(reset_down_adapter_left, reset_down_right_stacked)
    ).astype(jnp.bfloat16)
    return (
        mixed,
        grad_tokens,
        grad_gain,
        grad_shift,
        grad_a,
        grad_a_ff,
        grad_b,
        grad_b_ff,
        new_mean_a,
        new_square_a,
        new_mean_a_ff,
        new_square_a_ff,
        new_mean_b,
        new_square_b,
        new_mean_b_ff,
        new_square_b_ff,
        folded_input_weights,
        folded_down_weight,
    )


def solution(mesh):
    in_specs = (
        P("dp", "blk", None),
        P("dp", "blk", None),
        P("dp", "blk"),
        P(),
        P("dp", None),
        P(),
        P("dp", None),
        P(),
        P(),
        P(),
        P("dp", None),
        P("dp", None),
        P(None, "dp"),
        P(None, "dp"),
        P("dp", None),
        P("dp", None),
        P(None, "dp"),
        P(None, "dp"),
        P("dp", None),
        P("dp", None),
        P(None, "dp"),
        P(None, "dp"),
        P("dp", None),
        P("dp", None),
        P(None, "dp"),
        P(None, "dp"),
    )
    out_specs = (
        P("dp", "blk", None),
        P("dp", "blk", None),
        P(),
        P(),
        P("dp", None),
        P("dp", None),
        P(None, "dp"),
        P(None, "dp"),
        P("dp", None),
        P("dp", None),
        P("dp", None),
        P("dp", None),
        P(None, "dp"),
        P(None, "dp"),
        P(None, "dp"),
        P(None, "dp"),
        P("dp", None),
        P("dp", None),
    )
    return jax.shard_map(body, mesh=mesh, in_specs=in_specs, out_specs=out_specs, check_vma=False)
```

profile of v0, /device:TPU:0, one launch (start us, length us, event | category | flops | bytes accessed | tf_op | source)
XLA Modules:
  0.0 990.2 jit_solution(3469510999970349865)
XLA Ops:
  12.5 12.9 %all_gather.45 = bf16[1024,384]{1,0:T(8,128)(2,1)} all-gather(bf16[128,384]{1,0:T(8,128)(2,1)S(1)} %convert_element_type.174), channel_id=1, replica_groups=mesh['dp'=8,'blk'=4] {'dp'}, dimensions={0}, use_global_device_ids=true | all-gather | bytes 884736 | tf_op jit(solution)/shard_map/all_gather | solution.py:163
  30.0 72.5 %all-gather.10.cloned.1.call-done = bf16[1024,8192]{1,0:T(8,128)(2,1)} async-done(((bf16[128,8192]{1,0:T(8,128)(2,1)}), bf16[1024,8192]{1,0:T(8,128)(2,1)}) %all-gather.10.cloned.1.call-update) | async-done | bytes 16777232 | tf_op jit(solution)/shard_map/all_gather | solution.py:161
  112.8 20.2 %all-gather.12.cloned.1.call-done = bf16[128,8192]{1,0:T(8,128)(2,1)} async-done(((bf16[128,1024]{1,0:T(8,128)(2,1)}), bf16[128,8192]{1,0:T(8,128)(2,1)}) %all-gather.12.cloned.1.call-update) | async-done | bytes 2097168 | tf_op jit(solution)/shard_map/all_gather | solution.py:165
  168.0 10.3 %all_gather.51 = bf16[128,1024]{1,0:T(8,128)(2,1)S(1)} all-gather(bf16[128,128]{1,0:T(8,128)(2,1)} %convert_element_type.194), channel_id=1, replica_groups=mesh['dp'=8,'blk'=4] {'dp'}, dimensions={1}, use_global_device_ids=true | all-gather | bytes 294912 | tf_op jit(solution)/shard_map/all_gather | solution.py:166
  190.3 12.6 %fusion.136 = f32[768,4096]{1,0:T(8,128)} fusion(bf16[768,1024]{1,0:T(8,128)(2,1)S(1)} %fusion.28, bf16[4096,1024]{1,0:T(8,128)(2,1)} %all-gather.18.cloned.1.call-done), kind=kOutput, calls=%fused_computation.232 | convolution fusion | flops 6442450944 | bytes 22544384 | tf_op jit(solution)/shard_map/dot_general | solution.py:24
  231.5 31.8 %multiply_convert_fusion.2 = (bf16[768,4096]{1,0:T(8,128)(2,1)}, f32[768,4096]{1,0:T(8,128)}, f32[768,4096]{1,0:T(8,128)}) fusion(bf16[768,128]{1,0:T(8,128)(2,1)S(1)} %copy-done.54, bf16[128,8192]{1,0:T(8,128)(2,1)S(1)} %copy-done.56, f32[768,4096]{1,0:T(8,128)S(1)} %fusion.19, f32[4096]{0:T(1024)S(1)} %copy-done.84), kind=kOutput, calls=%fused_computation.15 | convolution fusion | flops 1019215872 | bytes 45301760 | tf_op jit(solution)/shard_map/dot_general | solution.py:20
  263.4 17.3 %add_convert_fusion = bf16[768,4096]{1,0:T(8,128)(2,1)} fusion(f32[768,4096]{1,0:T(8,128)} %get-tuple-element.99, f32[768,4096]{1,0:T(8,128)} %fusion.136, f32[768,4096]{1,0:T(8,128)} %get-tuple-element.136, bf16[768,128]{1,0:T(8,128)(2,1)} %fusion.69, bf16[4096,128]{1,0:T(8,128)(2,1)} %all-gather.20.cloned.1.call-done), kind=kOutput, calls=%fused_computation.14 | convolution fusion | flops 852492288 | bytes 45285376 | tf_op jit(solution)/shard_map/dot_general | solution.py:24
  298.8 12.6 %fusion.135 = f32[768,1024]{1,0:T(8,128)} fusion(bf16[768,4096]{1,0:T(8,128)(2,1)} %get-tuple-element.98, bf16[4096,1024]{1,0:T(8,128)(2,1)} %all-gather.18.cloned.1.call-done), kind=kOutput, calls=%fused_computation.231 | convolution fusion | flops 6442450944 | bytes 17825792 | tf_op jit(solution)/shard_map/dot_general | solution.py:20
  311.4 21.1 %all-gather.16.cloned.1.call-done = bf16[3,1024,1024]{1,2,0:T(8,128)(2,1)} async-done(((bf16[3,256,1024]{1,2,0:T(8,128)(2,1)}), bf16[3,1024,1024]{1,2,0:T(8,128)(2,1)}) %all-gather.16.cloned.1.call-update) | async-done | bytes 6291472 | tf_op jit(solution)/shard_map/all_gather | solution.py:193
  332.5 21.8 %select_reduce_fusion = (f32[3,16,256]{2,1,0:T(8,128)S(1)}, f32[3,16,256,1024]{3,2,1,0:T(8,128)}) fusion(pred[256,1024]{1,0:T(8,128)(4,1)S(1)} %copy-done.5, bf16[3,1024,16,64]{1,3,2,0:T(8,128)(2,1)} %bitcast.174, bf16[3,256,16,48]{1,3,2,0:T(8,128)(2,1)S(1)} %copy-done.14, bf16[3,256,16,8]{1,3,2,0:T(8,128)(2,1)S(1)} %get-tuple-element.124, ...), kind=kOutput, calls=%fused_computation.4 | convolution fusion | flops 1653067776 | bytes 58507264 | tf_op jit(solution)/shard_map/sqhe,skhe->shqk/dot_general | solution.py:199
  354.3 23.0 %fusion.1 = f32[3,16,256]{2,1,0:T(8,128)S(1)} fusion(f32[3,16,256,1024]{3,2,1,0:T(8,128)} %get-tuple-element.135, f32[3,16,256]{2,1,0:T(8,128)S(1)} %broadcast_maximum_fusion, pred[256,1024]{1,0:T(8,128)(4,1)S(1)} %copy-done.5), kind=kLoop, calls=%fused_computation.6 | loop fusion | flops 62902272 | bytes 50692096 | tf_op jit(solution)/shard_map/reduce_sum | solution.py:206
  377.3 20.7 %all_gather.53 = bf16[3,16,1024]{2,1,0:T(8,128)(2,1)S(1)} all-gather(bf16[3,16,256]{2,1,0:T(8,128)(2,1)S(1)} %get-tuple-element.96), channel_id=1, replica_groups=mesh['dp'=8,'blk'=4] {'blk'}, dimensions={2}, use_global_device_ids=true | all-gather | bytes 122880 | tf_op jit(solution)/shard_map/all_gather | solution.py:254
  398.0 50.5 %all-gather.14.cloned.1.call-done = bf16[3,1024,1024]{1,2,0:T(8,128)(2,1)} async-done(((bf16[3,256,1024]{1,2,0:T(8,128)(2,1)}), bf16[3,1024,1024]{1,2,0:T(8,128)(2,1)}) %all-gather.14.cloned.1.call-update) | async-done | bytes 6291472 | tf_op jit(solution)/shard_map/all_gather | solution.py:194
  448.5 23.5 %multiply_reduce_fusion = (f32[3,256,16]{1,2,0:T(8,128)S(1)}, bf16[3,256,16,64]{1,3,2,0:T(8,128)(2,1)}) fusion(bf16[3,256,16,64]{1,3,2,0:T(8,128)(2,1)S(1)} %copy-done.39, f32[3,256,16]{1,2,0:T(8,128)S(1)} %bitcast.202, bf16[3,1024,16,64]{1,3,2,0:T(8,128)(2,1)} %bitcast.218, f32[3,16,256,1024]{3,2,1,0:T(8,128)} %get-tuple-element.135, ...), kind=kOutput, calls=%fused_computation.86 | convolution fusion | flops 1677447168 | bytes 60178432 | tf_op jit(solution)/shard_map/shqk,skhe->sqhe/dot_general | solution.py:207
  472.1 28.8 %multiply_bitcast_fusion.1 = f32[3,256,16,64]{1,3,2,0:T(8,128)} fusion(bf16[3,1024,16,64]{1,3,2,0:T(8,128)(2,1)} %bitcast.175, f32[3,16,256,1024]{3,2,1,0:T(8,128)} %get-tuple-element.135, bf16[3,256,16,64]{1,3,2,0:T(8,128)(2,1)S(1)} %copy-done.39, bf16[3,1024,16,64]{1,3,2,0:T(8,128)(2,1)} %bitcast.219, f32[3,16,256]{2,1,0:T(8,128)S(1)} %bitcast.211, ...), kind=kOutput, calls=%fused_computation.85 | convolution fusion | flops 3297509376 | bytes 67993600 | tf_op jit(solution)/shard_map/shqk,skhe->sqhe/dot_general | solution.py:251
  500.9 27.6 %all_gather.55 = bf16[3,16,1024]{2,1,0:T(8,128)(2,1)S(1)} all-gather(bf16[3,16,256]{2,1,0:T(8,128)(2,1)S(1)} %bitcast_convert_fusion), channel_id=1, replica_groups=mesh['dp'=8,'blk'=4] {'blk'}, dimensions={2}, use_global_device_ids=true | all-gather | bytes 122880 | tf_op jit(solution)/shard_map/all_gather | solution.py:257
  529.2 35.5 %all-gather.22.cloned.1.call-done = bf16[3,1024,1024]{1,2,0:T(8,128)(2,1)} async-done(((bf16[3,256,1024]{1,2,0:T(8,128)(2,1)}), bf16[3,1024,1024]{1,2,0:T(8,128)(2,1)}) %all-gather.22.cloned.1.call-update) | async-done | bytes 6291472 | tf_op jit(solution)/shard_map/all_gather | solution.py:259
  564.7 22.0 %fusion.134 = f32[3,16,1024,256]{3,2,1,0:T(8,128)} fusion(bf16[3,1024,16,64]{1,3,2,0:T(8,128)(2,1)} %bitcast.179, bf16[3,256,16,48]{1,3,2,0:T(8,128)(2,1)S(1)} %copy-done.13, bf16[3,256,16,8]{1,3,2,0:T(8,128)(2,1)S(1)} %copy-done.36, bf16[3,256,16,8]{1,3,2,0:T(8,128)(2,1)S(1)} %copy-done.34), kind=kOutput, calls=%fused_computation.230 | convolution fusion | flops 1615331328 | bytes 58195968 | tf_op jit(solution)/shard_map/sqhe,skhe->shqk/dot_general | solution.py:265
  586.7 93.3 %all-gather.24.cloned.1.call-done = bf16[3,1024,1024]{2,1,0:T(8,128)(2,1)} async-done(((bf16[3,256,1024]{2,1,0:T(8,128)(2,1)}), bf16[3,1024,1024]{2,1,0:T(8,128)(2,1)}) %all-gather.24.cloned.1.call-update) | async-done | bytes 6291472 | tf_op jit(solution)/shard_map/all_gather | solution.py:260
  688.7 20.5 %fusion.64 = bf16[3,256,16,64]{1,3,2,0:T(8,128)(2,1)} fusion(bf16[3,1024,16,64]{1,3,2,0:T(8,128)(2,1)} %bitcast.189, f32[3,16,1024,256]{3,2,1,0:T(8,128)} %fusion.134, f32[3,16,1024]{2,1,0:T(8,128)S(1)} %convert_element_type.203, pred[1024,256]{1,0:T(8,128)(4,1)S(1)} %copy-done.60), kind=kOutput, calls=%fused_computation.97 | convolution fusion | flops 1661730816 | bytes 58654720 | tf_op jit(solution)/shard_map/shqk,sqhe->skhe/dot_general | solution.py:270
  709.2 28.0 %multiply_bitcast_fusion = f32[3,256,16,64]{1,3,2,0:T(8,128)} fusion(bf16[3,1024,16,64]{1,3,2,0:T(8,128)(2,1)} %bitcast.180, f32[3,16,1024,256]{3,2,1,0:T(8,128)} %fusion.134, bf16[3,1024,16,64]{1,3,2,0:T(8,128)(2,1)} %bitcast.190, bf16[3,256,16,64]{1,3,2,0:T(8,128)(2,1)} %bitcast.191, f32[3,16,1024]{2,1,0:T(8,128)} %convert_element_type.206, ...), kind=kOutput, calls=%fused_computation.83 | convolution fusion | flops 3297509376 | bytes 68288512 | tf_op jit(solution)/shard_map/shqk,sqhe->skhe/dot_general | solution.py:276
  772.9 13.2 %fusion.128 = (f32[1024]{0:T(1024)S(1)}, f32[768]{0:T(1024)S(1)}, f32[768]{0:T(1024)S(1)}, f32[1024]{0:T(1024)S(1)}, f32[768,1024]{1,0:T(8,128)S(1)}) fusion(f32[1024]{0:T(1024)S(1)} %bitcast.208, f32[768]{0:T(1024)S(1)} %copy-done.71, bf16[3,256,1024]{2,1,0:T(8,128)(2,1)S(1)} %copy-done.1, f32[768,1024]{1,0:T(8,128)S(1)} %convolution_add_fusion, ...), kind=kOutput, calls=%fused_computation.225 | convolution fusion | flops 6451097600 | bytes 25715712 | tf_op jit(solution)/shard_map/dot_general | solution.py:24
  789.1 39.3 %all-reduce.6 = (f32[2,1024]{1,0:T(2,128)}, f32[2,1024]{1,0:T(2,128)}) all-reduce(f32[2,1024]{1,0:T(2,128)S(1)} %pad_maximum_fusion.2, f32[2,1024]{1,0:T(2,128)S(1)} %pad_maximum_fusion.3), channel_id=1, replica_groups=mesh['dp'=8,'blk'=4] {'dp','blk'}, use_global_device_ids=true, to_apply=%region_12.13 | all-reduce | flops 4096 | bytes 32768 | tf_op jit(solution)/shard_map/psum | solution.py:298
  836.6 103.6 %all-reduce.10.cloned.1.call-done = (f32[1024,384]{0,1:T(8,128)}, f32[4096,128]{1,0:T(8,128)}, f32[128,8192]{1,0:T(8,128)}, f32[128,1024]{1,0:T(8,128)}) async-done(((f32[1024,384]{0,1:T(8,128)}, f32[4096,128]{1,0:T(8,128)}, f32[128,8192]{1,0:T(8,128)}, f32[128,1024]{1,0:T(8,128)}), (f32[1024,384]{0,1:T(8,128)}, f32[4096,128]{1,0:T(8,128)}, f32[128,8192]{1,0:T(8,128)}, ...) | async-done | bytes 8388624 | tf_op jit(solution)/shard_map/psum | solution.py:298
  (329 shorter events, 211.8 us)
Async XLA Ops:
  7.2 95.3 %all-gather.10.cloned.1.call-start = ((), (), s32[]{:S(2)}) async-start(), calls=%async_computation | async-start | bytes 18874368 | tf_op jit(solution)/shard_map/all_gather | solution.py:161
  8.0 125.0 %all-gather.12.cloned.1.call-start = ((), (), s32[]{:S(2)}) async-start(), calls=%async_computation.1 | async-start | bytes 2359296 | tf_op jit(solution)/shard_map/all_gather | solution.py:165
  9.9 180.5 %all-gather.18.cloned.1.call-start = ((), (), s32[]{:S(2)}) async-start(), calls=%async_computation.4 | async-start | bytes 9437184 | tf_op jit(solution)/shard_map/all_gather | solution.py:162
  10.6 252.8 %all-gather.20.cloned.1.call-start = ((), (), s32[]{:S(2)}) async-start(), calls=%async_computation.5 | async-start | bytes 1179648 | tf_op jit(solution)/shard_map/all_gather | solution.py:164
  11.4 321.1 %all-gather.16.cloned.1.call-start = ((), (), s32[]{:S(2)}) async-start(), calls=%async_computation.3 | async-start | bytes 7864320 | tf_op jit(solution)/shard_map/all_gather | solution.py:193
  28.1 84.6 %copy-start.21 = (bf16[768,1024]{1,0:T(8,128)(2,1)}, bf16[768,1024]{1,0:T(8,128)(2,1)S(1)}, u32[]{:S(2)}) copy-start(bf16[768,1024]{1,0:T(8,128)(2,1)S(1)} %get-tuple-element.112) | copy-start | bytes 4718596
  29.9 103.1 %copy-start.45 = (bf16[768,128]{1,0:T(8,128)(2,1)}, bf16[768,128]{1,0:T(8,128)(2,1)S(1)}, u32[]{:S(2)}) copy-start(bf16[768,128]{1,0:T(8,128)(2,1)S(1)} %convolution_convert_fusion.3) | copy-start | bytes 589828
  30.0 121.2 %copy-start.66 = (f32[256,8]{0,1:T(8,128)}, f32[256,8]{0,1:T(8,128)S(1)}, u32[]{:S(2)}) copy-start(f32[256,8]{0,1:T(8,128)S(1)} %get-tuple-element.132) | copy-start | bytes 24580
  30.0 121.2 %copy-start.68 = (f32[256,8]{0,1:T(8,128)}, f32[256,8]{0,1:T(8,128)S(1)}, u32[]{:S(2)}) copy-start(f32[256,8]{0,1:T(8,128)S(1)} %get-tuple-element.133) | copy-start | bytes 24580
  154.7 293.8 %all-gather.14.cloned.1.call-start = ((), (), s32[]{:S(2)}) async-start(), calls=%async_computation.2 | async-start | bytes 7864320 | tf_op jit(solution)/shard_map/all_gather | solution.py:194
  158.6 406.2 %all-gather.22.cloned.1.call-start = ((), (), s32[]{:S(2)}) async-start(), calls=%async_computation.6 | async-start | bytes 7864320 | tf_op jit(solution)/shard_map/all_gather | solution.py:259
  185.2 103.5 %copy-start.6 = (bf16[768,1024]{1,0:T(8,128)(2,1)}, bf16[768,1024]{1,0:T(8,128)(2,1)S(1)}, u32[]{:S(2)}) copy-start(bf16[768,1024]{1,0:T(8,128)(2,1)S(1)} %fusion.28) | copy-start | bytes 4718596
  221.8 458.3 %all-gather.24.cloned.1.call-start = ((), (), s32[]{:S(2)}) async-start(), calls=%async_computation.7 | async-start | bytes 7864320 | tf_op jit(solution)/shard_map/all_gather | solution.py:260
  298.7 641.4 %all-reduce.10.cloned.1.call-start = ((), (), s32[]{:S(2)}) async-start(), calls=%async_computation.9 | async-start | bytes 16777216 | tf_op jit(solution)/shard_map/psum | solution.py:298
  354.3 94.2 %copy-start.39 = (bf16[3,256,16,64]{1,3,2,0:T(8,128)(2,1)S(1)}, bf16[3,256,16,64]{1,3,2,0:T(8,128)(2,1)}, u32[]{:S(2)}) copy-start(bf16[3,256,16,64]{1,3,2,0:T(8,128)(2,1)} %copy.77) | copy-start | bytes 4718596
  398.0 290.7 %copy-start.64 = (f32[3,16,1024]{2,1,0:T(8,128)}, f32[3,16,1024]{2,1,0:T(8,128)S(1)}, u32[]{:S(2)}) copy-start(f32[3,16,1024]{2,1,0:T(8,128)S(1)} %convert_element_type.203) | copy-start | bytes 589828
  500.9 63.8 %copy-start.34 = (bf16[3,256,16,8]{1,3,2,0:T(8,128)(2,1)S(1)}, bf16[3,256,16,8]{1,3,2,0:T(8,128)(2,1)}, u32[]{:S(2)}) copy-start(bf16[3,256,16,8]{1,3,2,0:T(8,128)(2,1)} %copy-done.33) | copy-start | bytes 589828
  500.9 63.8 %copy-start.36 = (bf16[3,256,16,8]{1,3,2,0:T(8,128)(2,1)S(1)}, bf16[3,256,16,8]{1,3,2,0:T(8,128)(2,1)}, u32[]{:S(2)}) copy-start(bf16[3,256,16,8]{1,3,2,0:T(8,128)(2,1)} %copy-done.35) | copy-start | bytes 589828
  586.7 102.0 %copy-start.60 = (pred[1024,256]{1,0:T(8,128)(4,1)S(1)}, pred[1024,256]{1,0:T(8,128)(4,1)}, u32[]{:S(2)}) copy-start(pred[1024,256]{1,0:T(8,128)(4,1)} %iota_compare_fusion) | copy-start | bytes 786436
  761.6 215.2 %all-gather.26.cloned.1.call-start = ((), (), s32[]{:S(2)}) async-start(), calls=%async_computation.8 | async-start | bytes 2359296 | tf_op jit(solution)/shard_map/all_gather | solution.py:321
  836.6 106.2 %copy-start.41 = (bf16[128,1024]{1,0:T(8,128)(2,1)S(1)}, bf16[128,1024]{1,0:T(8,128)(2,1)}, u32[]{:S(2)}) copy-start(bf16[128,1024]{1,0:T(8,128)(2,1)} %copy-done.40) | copy-start | bytes 786436
  836.6 106.2 %copy-start.53 = (bf16[768,128]{1,0:T(8,128)(2,1)S(1)}, bf16[768,128]{1,0:T(8,128)(2,1)}, u32[]{:S(2)}) copy-start(bf16[768,128]{1,0:T(8,128)(2,1)} %copy-done.52) | copy-start | bytes 589828
  836.6 106.2 %copy-start.82 = (f32[1024]{0:T(1024)S(1)}, f32[1024]{0:T(1024)}, u32[]{:S(2)}) copy-start(f32[1024]{0:T(1024)} %convert_element_type.191) | copy-start | bytes 12292
  836.6 106.2 %copy-start.83 = (f32[1024]{0:T(1024)S(1)}, f32[1024]{0:T(1024)}, u32[]{:S(2)}) copy-start(f32[1024]{0:T(1024)} %slice_convert_fusion.2) | copy-start | bytes 12292
  (81 other events, 823.4 us)
Sparse Core Ops, SparseCore 0:
  9.9 92.5 all-gather.9
  105.0 27.8 all-gather.11
  134.8 55.4 all-gather.17
  192.6 23.4 all-gather.19
  217.6 114.8 all-gather.15
  333.9 114.6 all-gather.13
  450.1 114.6 all-gather.21
  566.3 113.7 all-gather.23
  761.7 178.4 all-reduce.9
  942.9 28.6 all-gather.25
where the time goes:
time: 999 us; the launch traced here: 990 us
  waiting for transfers between devices  400 us (40%)
  matrix products  326 us (33%)
  blocking collectives  121 us (12%)
  other arithmetic  68.4 us (7%)
  local copies, waits for them, and re-layouts  58.5 us (6%)
  between operations  15.7 us (2%)
    psum x1, waiting for transfers between devices, body(): lax.psum((grad_a_part, grad_a_ffp, grad_b_part, grad_b_ffp, gain_part, sh...  104 us
    all_gather x1, waiting for transfers between devices, body(): lax.all_gather(grad_att.reshape(seqs, span, width), 'blk', axis=1, tiled=...  93.3 us
    dot_general x12, matrix products, matrix_product(): return jnp.dot(left, right, preferred_element_type=jnp.float32)  91.1 us
    dot_general x12, matrix products, product_right_transposed(): lax.dot_general(left, right, (((1,), (1,)), ((), ())), preferred_element_...  72.7 us
    all_gather x1, waiting for transfers between devices, body(): lax.all_gather(shards[0], 'dp', axis=0, tiled=True)  72.5 us
    all_gather x1, waiting for transfers between devices, body(): value_piece = lax.all_gather(value_send, 'blk', axis=1, tiled=True)  50.5 us
    psum x1, blocking collectives, body(): lax.psum((grad_a_part, grad_a_ffp, grad_b_part, grad_b_ffp, gain_part, sh...  39.3 us
    all_gather x1, waiting for transfers between devices, body(): lax.all_gather(query_b.reshape(seqs, span, width), 'blk', axis=1, tiled=T...  35.5 us
  transfers between devices with their start and end apart: 10, of which 8 were waited for; matrix products, arithmetic and copies ran while one was open for 36% of the time, Pallas kernels for 0%

commit v1 on v0

--- a/solution.py
+++ b/solution.py
@@ -14,6 +14,11 @@
 masked_score = -1e30
 first_fix = 1.0 - (0.9**10) ** 10
 second_fix = 1.0 - (0.999**10) ** 10
+
+
+def axis_by_axis(array, one, other):
+    inner = lax.psum(array, one)
+    return lax.psum(inner, other)
 
 
 def matrix_product(left, right):
@@ -295,8 +300,8 @@
     shift_part = jnp.stack([back_one[2], back_two[2]])
     grad_a_part = jnp.concatenate([grad_a_qkv, grad_a_att, grad_a_up], axis=1)
     grad_b_part = jnp.concatenate([grad_b_qkv, grad_b_att, grad_b_up], axis=1)
-    summed = lax.psum(
-        (grad_a_part, grad_a_ffp, grad_b_part, grad_b_ffp, gain_part, shift_part), ("dp", "blk")
+    summed = axis_by_axis(
+        (grad_a_part, grad_a_ffp, grad_b_part, grad_b_ffp, gain_part, shift_part), "blk", "dp"
     )
     owner = lax.axis_index("dp")
     grad_a = lax.dynamic_slice_in_dim(summed[0], owner * adapt_a.shape[0], adapt_a.shape[0], 0)

time: 999 us -> 1240 us (1.24)
  waiting for transfers between devices: 400 us -> 641 us
    psum x1 -> x2, waiting for transfers between devices: 104 us -> 320 us  [the longest x1 263 us: axis_by_axis(): inner = lax.psum(array, one)]
    all_gather x1, waiting for transfers between devices: 21.1 us -> 36.8 us  [body(): key_piece = lax.all_gather(key_send, 'blk', axis=1, tiled=True)]
    psum x1 -> x2, blocking collectives: 39.3 us -> 41.4 us  [the longest x1 24.1 us: axis_by_axis(): return lax.psum(inner, other)]
  transfers between devices with their start and end apart: 10 -> 11, of which waited for: 8 -> 9; matrix products, arithmetic and copies ran while one was open for 36% -> 29% of each run, Pallas kernels for 0% -> 0%
where the time goes in v1:
time: 1240 us; the launch traced here: 1230 us
  waiting for transfers between devices  641 us (52%)
  matrix products  326 us (26%)
  blocking collectives  122 us (10%)
  other arithmetic  70.8 us (6%)
  local copies, waits for them, and re-layouts  54.5 us (4%)
  between operations  15.5 us (1%)
    psum x1, waiting for transfers between devices, axis_by_axis(): inner = lax.psum(array, one)  263 us
    all_gather x1, waiting for transfers between devices, body(): lax.all_gather(grad_att.reshape(seqs, span, width), 'blk', axis=1, tiled=...  93.4 us
    dot_general x12, matrix products, matrix_product(): return jnp.dot(left, right, preferred_element_type=jnp.float32)  90.4 us
    dot_general x12, matrix products, product_right_transposed(): lax.dot_general(left, right, (((1,), (1,)), ((), ())), preferred_element_...  72.8 us
    all_gather x1, waiting for transfers between devices, body(): lax.all_gather(shards[0], 'dp', axis=0, tiled=True)  72.5 us
    psum x1, waiting for transfers between devices, axis_by_axis(): return lax.psum(inner, other)  57.5 us
    all_gather x1, waiting for transfers between devices, body(): value_piece = lax.all_gather(value_send, 'blk', axis=1, tiled=True)  50.5 us
    all_gather x1, waiting for transfers between devices, body(): key_piece = lax.all_gather(key_send, 'blk', axis=1, tiled=True)  36.8 us
  transfers between devices with their start and end apart: 11, of which 9 were waited for; matrix products, arithmetic and copies ran while one was open for 29% of the time, Pallas kernels for 0%

profile of v1, /device:TPU:0, one launch (start us, length us, event | category | flops | bytes accessed | tf_op | source)
XLA Modules:
  0.0 1231.3 jit_solution(4336502659930537610)
XLA Ops:
  12.5 12.9 %all_gather.45 = bf16[1024,384]{1,0:T(8,128)(2,1)} all-gather(bf16[128,384]{1,0:T(8,128)(2,1)S(1)} %convert_element_type.174), channel_id=1, replica_groups=mesh['dp'=8,'blk'=4] {'dp'}, dimensions={0}, use_global_device_ids=true | all-gather | bytes 884736 | tf_op jit(solution)/shard_map/all_gather | solution.py:168
  30.0 72.5 %all-gather.10.cloned.1.call-done = bf16[1024,8192]{1,0:T(8,128)(2,1)} async-done(((bf16[128,8192]{1,0:T(8,128)(2,1)}), bf16[1024,8192]{1,0:T(8,128)(2,1)}) %all-gather.10.cloned.1.call-update) | async-done | bytes 16777232 | tf_op jit(solution)/shard_map/all_gather | solution.py:166
  112.8 20.2 %all-gather.12.cloned.1.call-done = bf16[128,8192]{1,0:T(8,128)(2,1)} async-done(((bf16[128,1024]{1,0:T(8,128)(2,1)}), bf16[128,8192]{1,0:T(8,128)(2,1)}) %all-gather.12.cloned.1.call-update) | async-done | bytes 2097168 | tf_op jit(solution)/shard_map/all_gather | solution.py:170
  190.0 12.6 %fusion.136 = f32[768,4096]{1,0:T(8,128)} fusion(bf16[768,1024]{1,0:T(8,128)(2,1)S(1)} %fusion.28, bf16[4096,1024]{1,0:T(8,128)(2,1)} %all-gather.18.cloned.1.call-done), kind=kOutput, calls=%fused_computation.232 | convolution fusion | flops 6442450944 | bytes 22544384 | tf_op jit(solution)/shard_map/dot_general | solution.py:29
  231.2 31.9 %multiply_convert_fusion.2 = (bf16[768,4096]{1,0:T(8,128)(2,1)}, f32[768,4096]{1,0:T(8,128)}, f32[768,4096]{1,0:T(8,128)}) fusion(bf16[768,128]{1,0:T(8,128)(2,1)S(1)} %copy-done.57, bf16[128,8192]{1,0:T(8,128)(2,1)S(1)} %copy-done.59, f32[768,4096]{1,0:T(8,128)S(1)} %fusion.19, f32[4096]{0:T(1024)S(1)} %copy-done.95), kind=kOutput, calls=%fused_computation.15 | convolution fusion | flops 1019215872 | bytes 45301760 | tf_op jit(solution)/shard_map/dot_general | solution.py:25
  263.1 17.2 %add_convert_fusion = bf16[768,4096]{1,0:T(8,128)(2,1)} fusion(f32[768,4096]{1,0:T(8,128)} %get-tuple-element.105, f32[768,4096]{1,0:T(8,128)} %fusion.136, f32[768,4096]{1,0:T(8,128)} %get-tuple-element.142, bf16[768,128]{1,0:T(8,128)(2,1)} %fusion.69, bf16[4096,128]{1,0:T(8,128)(2,1)} %all-gather.20.cloned.1.call-done), kind=kOutput, calls=%fused_computation.14 | convolution fusion | flops 852492288 | bytes 45285376 | tf_op jit(solution)/shard_map/dot_general | solution.py:29
  295.3 36.8 %all-gather.16.cloned.1.call-done = bf16[3,1024,1024]{1,2,0:T(8,128)(2,1)} async-done(((bf16[3,256,1024]{1,2,0:T(8,128)(2,1)}), bf16[3,1024,1024]{1,2,0:T(8,128)(2,1)}) %all-gather.16.cloned.1.call-update) | async-done | bytes 6291472 | tf_op jit(solution)/shard_map/all_gather | solution.py:198
  332.1 21.8 %select_reduce_fusion = (f32[3,16,256]{2,1,0:T(8,128)S(1)}, f32[3,16,256,1024]{3,2,1,0:T(8,128)}) fusion(pred[256,1024]{1,0:T(8,128)(4,1)S(1)} %copy-done.5, bf16[3,1024,16,64]{1,3,2,0:T(8,128)(2,1)} %bitcast.174, bf16[3,256,16,48]{1,3,2,0:T(8,128)(2,1)S(1)} %copy-done.14, bf16[3,256,16,8]{1,3,2,0:T(8,128)(2,1)S(1)} %get-tuple-element.130, ...), kind=kOutput, calls=%fused_computation.4 | convolution fusion | flops 1653067776 | bytes 58507264 | tf_op jit(solution)/shard_map/sqhe,skhe->shqk/dot_general | solution.py:204
  354.0 23.0 %fusion.1 = f32[3,16,256]{2,1,0:T(8,128)S(1)} fusion(f32[3,16,256,1024]{3,2,1,0:T(8,128)} %get-tuple-element.141, f32[3,16,256]{2,1,0:T(8,128)S(1)} %broadcast_maximum_fusion, pred[256,1024]{1,0:T(8,128)(4,1)S(1)} %copy-done.5), kind=kLoop, calls=%fused_computation.6 | loop fusion | flops 62902272 | bytes 50692096 | tf_op jit(solution)/shard_map/reduce_sum | solution.py:211
  377.0 20.7 %all_gather.53 = bf16[3,16,1024]{2,1,0:T(8,128)(2,1)S(1)} all-gather(bf16[3,16,256]{2,1,0:T(8,128)(2,1)S(1)} %get-tuple-element.102), channel_id=1, replica_groups=mesh['dp'=8,'blk'=4] {'blk'}, dimensions={2}, use_global_device_ids=true | all-gather | bytes 122880 | tf_op jit(solution)/shard_map/all_gather | solution.py:259
  397.7 50.5 %all-gather.14.cloned.1.call-done = bf16[3,1024,1024]{1,2,0:T(8,128)(2,1)} async-done(((bf16[3,256,1024]{1,2,0:T(8,128)(2,1)}), bf16[3,1024,1024]{1,2,0:T(8,128)(2,1)}) %all-gather.14.cloned.1.call-update) | async-done | bytes 6291472 | tf_op jit(solution)/shard_map/all_gather | solution.py:199
  448.2 23.8 %multiply_reduce_fusion = (f32[3,256,16]{1,2,0:T(8,128)S(1)}, bf16[3,256,16,64]{1,3,2,0:T(8,128)(2,1)}) fusion(bf16[3,256,16,64]{1,3,2,0:T(8,128)(2,1)S(1)} %copy-done.37, f32[3,256,16]{1,2,0:T(8,128)S(1)} %bitcast.204, bf16[3,1024,16,64]{1,3,2,0:T(8,128)(2,1)} %bitcast.220, f32[3,16,256,1024]{3,2,1,0:T(8,128)} %get-tuple-element.141, ...), kind=kOutput, calls=%fused_computation.86 | convolution fusion | flops 1677447168 | bytes 60178432 | tf_op jit(solution)/shard_map/shqk,skhe->sqhe/dot_general | solution.py:212
  472.0 28.8 %multiply_bitcast_fusion.1 = f32[3,256,16,64]{1,3,2,0:T(8,128)} fusion(bf16[3,1024,16,64]{1,3,2,0:T(8,128)(2,1)} %bitcast.175, f32[3,16,256,1024]{3,2,1,0:T(8,128)} %get-tuple-element.141, bf16[3,256,16,64]{1,3,2,0:T(8,128)(2,1)S(1)} %copy-done.37, bf16[3,1024,16,64]{1,3,2,0:T(8,128)(2,1)} %bitcast.221, f32[3,16,256]{2,1,0:T(8,128)S(1)} %bitcast.213, ...), kind=kOutput, calls=%fused_computation.85 | convolution fusion | flops 3297509376 | bytes 67993600 | tf_op jit(solution)/shard_map/shqk,skhe->sqhe/dot_general | solution.py:256
  500.8 27.4 %all_gather.55 = bf16[3,16,1024]{2,1,0:T(8,128)(2,1)S(1)} all-gather(bf16[3,16,256]{2,1,0:T(8,128)(2,1)S(1)} %bitcast_convert_fusion), channel_id=1, replica_groups=mesh['dp'=8,'blk'=4] {'blk'}, dimensions={2}, use_global_device_ids=true | all-gather | bytes 122880 | tf_op jit(solution)/shard_map/all_gather | solution.py:262
  528.9 35.5 %all-gather.22.cloned.1.call-done = bf16[3,1024,1024]{1,2,0:T(8,128)(2,1)} async-done(((bf16[3,256,1024]{1,2,0:T(8,128)(2,1)}), bf16[3,1024,1024]{1,2,0:T(8,128)(2,1)}) %all-gather.22.cloned.1.call-update) | async-done | bytes 6291472 | tf_op jit(solution)/shard_map/all_gather | solution.py:264
  564.4 22.0 %fusion.134 = f32[3,16,1024,256]{3,2,1,0:T(8,128)} fusion(bf16[3,1024,16,64]{1,3,2,0:T(8,128)(2,1)} %bitcast.179, bf16[3,256,16,48]{1,3,2,0:T(8,128)(2,1)S(1)} %copy-done.13, bf16[3,256,16,8]{1,3,2,0:T(8,128)(2,1)S(1)} %copy-done.34, bf16[3,256,16,8]{1,3,2,0:T(8,128)(2,1)S(1)} %copy-done.32), kind=kOutput, calls=%fused_computation.230 | convolution fusion | flops 1615331328 | bytes 58195968 | tf_op jit(solution)/shard_map/sqhe,skhe->shqk/dot_general | solution.py:270
  586.4 93.4 %all-gather.24.cloned.1.call-done = bf16[3,1024,1024]{2,1,0:T(8,128)(2,1)} async-done(((bf16[3,256,1024]{2,1,0:T(8,128)(2,1)}), bf16[3,1024,1024]{2,1,0:T(8,128)(2,1)}) %all-gather.24.cloned.1.call-update) | async-done | bytes 6291472 | tf_op jit(solution)/shard_map/all_gather | solution.py:265
  688.4 20.5 %fusion.64 = bf16[3,256,16,64]{1,3,2,0:T(8,128)(2,1)} fusion(bf16[3,1024,16,64]{1,3,2,0:T(8,128)(2,1)} %bitcast.191, f32[3,16,1024,256]{3,2,1,0:T(8,128)} %fusion.134, f32[3,16,1024]{2,1,0:T(8,128)S(1)} %convert_element_type.203, pred[1024,256]{1,0:T(8,128)(4,1)S(1)} %copy-done.63), kind=kOutput, calls=%fused_computation.97 | convolution fusion | flops 1661730816 | bytes 58654720 | tf_op jit(solution)/shard_map/shqk,sqhe->skhe/dot_general | solution.py:275
  708.9 27.8 %multiply_bitcast_fusion = f32[3,256,16,64]{1,3,2,0:T(8,128)} fusion(bf16[3,1024,16,64]{1,3,2,0:T(8,128)(2,1)} %bitcast.180, f32[3,16,1024,256]{3,2,1,0:T(8,128)} %fusion.134, bf16[3,1024,16,64]{1,3,2,0:T(8,128)(2,1)} %bitcast.192, bf16[3,256,16,64]{1,3,2,0:T(8,128)(2,1)} %bitcast.196, f32[3,16,1024]{2,1,0:T(8,128)} %convert_element_type.206, ...), kind=kOutput, calls=%fused_computation.83 | convolution fusion | flops 3297509376 | bytes 68288512 | tf_op jit(solution)/shard_map/shqk,sqhe->skhe/dot_general | solution.py:281
  788.6 262.7 %all-reduce.15.cloned.1.call-done = (f32[1024,384]{0,1:T(8,128)}, f32[4096,128]{1,0:T(8,128)}, f32[128,8192]{1,0:T(8,128)}, f32[128,1024]{1,0:T(8,128)}) async-done(((f32[1024,384]{0,1:T(8,128)}, f32[4096,128]{1,0:T(8,128)}, f32[128,8192]{1,0:T(8,128)}, f32[128,1024]{1,0:T(8,128)}), (f32[1024,384]{0,1:T(8,128)}, f32[4096,128]{1,0:T(8,128)}, f32[128,8192]{1,0:T(8,128)}, ...) | async-done | bytes 8388624 | tf_op jit(solution)/shard_map/psum | solution.py:20
  1054.9 13.5 %fusion.128 = (f32[1024]{0:T(1024)S(1)}, f32[768]{0:T(1024)S(1)}, f32[768]{0:T(1024)S(1)}, f32[1024]{0:T(1024)S(1)}, f32[768,1024]{1,0:T(8,128)S(1)}) fusion(f32[1024]{0:T(1024)S(1)} %bitcast.210, f32[768]{0:T(1024)S(1)} %copy-done.76, bf16[3,256,1024]{2,1,0:T(8,128)(2,1)S(1)} %copy-done.1, f32[768,1024]{1,0:T(8,128)S(1)} %convolution_add_fusion, ...), kind=kOutput, calls=%fused_computation.225 | convolution fusion | flops 6451097600 | bytes 25715712 | tf_op jit(solution)/shard_map/dot_general | solution.py:29
  1073.2 17.3 %all-reduce.8 = (f32[2,1024]{1,0:T(2,128)}, f32[2,1024]{1,0:T(2,128)}) all-reduce(f32[2,1024]{1,0:T(2,128)} %pad_maximum_fusion.2, f32[2,1024]{1,0:T(2,128)} %pad_maximum_fusion.3), channel_id=1, replica_groups=mesh['dp'=8,'blk'=4] {'blk'}, use_global_device_ids=true, to_apply=%region_12.13 | all-reduce | flops 4096 | bytes 32768 | tf_op jit(solution)/shard_map/psum | solution.py:20
  1090.5 24.1 %all-reduce.6 = (f32[2,1024]{1,0:T(2,128)}, f32[2,1024]{1,0:T(2,128)}) all-reduce(f32[2,1024]{1,0:T(2,128)} %get-tuple-element.88, f32[2,1024]{1,0:T(2,128)} %get-tuple-element.89), channel_id=1, replica_groups=mesh['dp'=8,'blk'=4] {'dp'}, use_global_device_ids=true, to_apply=%region_13.14 | all-reduce | flops 4096 | bytes 32768 | tf_op jit(solution)/shard_map/psum | solution.py:21
  1124.4 57.5 %all-reduce.13.cloned.1.call-done = (f32[1024,384]{0,1:T(8,128)}, f32[4096,128]{1,0:T(8,128)}, f32[128,8192]{1,0:T(8,128)}, f32[128,1024]{1,0:T(8,128)}) async-done(((f32[1024,384]{0,1:T(8,128)}, f32[4096,128]{1,0:T(8,128)}, f32[128,8192]{1,0:T(8,128)}, f32[128,1024]{1,0:T(8,128)}), (f32[1024,384]{0,1:T(8,128)}, f32[4096,128]{1,0:T(8,128)}, f32[128,8192]{1,0:T(8,128)}, ...) | async-done | bytes 8388624 | tf_op jit(solution)/shard_map/psum | solution.py:21
  (360 shorter events, 241.6 us)
Async XLA Ops:
  7.2 95.3 %all-gather.10.cloned.1.call-start = ((), (), s32[]{:S(2)}) async-start(), calls=%async_computation | async-start | bytes 18874368 | tf_op jit(solution)/shard_map/all_gather | solution.py:166
  8.0 125.0 %all-gather.12.cloned.1.call-start = ((), (), s32[]{:S(2)}) async-start(), calls=%async_computation.1 | async-start | bytes 2359296 | tf_op jit(solution)/shard_map/all_gather | solution.py:170
  9.9 180.1 %all-gather.18.cloned.1.call-start = ((), (), s32[]{:S(2)}) async-start(), calls=%async_computation.4 | async-start | bytes 9437184 | tf_op jit(solution)/shard_map/all_gather | solution.py:167
  10.6 252.5 %all-gather.20.cloned.1.call-start = ((), (), s32[]{:S(2)}) async-start(), calls=%async_computation.5 | async-start | bytes 1179648 | tf_op jit(solution)/shard_map/all_gather | solution.py:169
  11.4 320.8 %all-gather.16.cloned.1.call-start = ((), (), s32[]{:S(2)}) async-start(), calls=%async_computation.3 | async-start | bytes 7864320 | tf_op jit(solution)/shard_map/all_gather | solution.py:198
  28.1 84.6 %copy-start.21 = (bf16[768,1024]{1,0:T(8,128)(2,1)}, bf16[768,1024]{1,0:T(8,128)(2,1)S(1)}, u32[]{:S(2)}) copy-start(bf16[768,1024]{1,0:T(8,128)(2,1)S(1)} %get-tuple-element.118) | copy-start | bytes 4718596
  29.9 103.1 %copy-start.43 = (bf16[768,128]{1,0:T(8,128)(2,1)}, bf16[768,128]{1,0:T(8,128)(2,1)S(1)}, u32[]{:S(2)}) copy-start(bf16[768,128]{1,0:T(8,128)(2,1)S(1)} %convolution_convert_fusion.3) | copy-start | bytes 589828
  30.0 121.3 %copy-start.71 = (f32[256,8]{0,1:T(8,128)}, f32[256,8]{0,1:T(8,128)S(1)}, u32[]{:S(2)}) copy-start(f32[256,8]{0,1:T(8,128)S(1)} %get-tuple-element.138) | copy-start | bytes 24580
  30.0 121.3 %copy-start.73 = (f32[256,8]{0,1:T(8,128)}, f32[256,8]{0,1:T(8,128)S(1)}, u32[]{:S(2)}) copy-start(f32[256,8]{0,1:T(8,128)S(1)} %get-tuple-element.139) | copy-start | bytes 24580
  154.7 293.5 %all-gather.14.cloned.1.call-start = ((), (), s32[]{:S(2)}) async-start(), calls=%async_computation.2 | async-start | bytes 7864320 | tf_op jit(solution)/shard_map/all_gather | solution.py:199
  158.5 405.9 %all-gather.22.cloned.1.call-start = ((), (), s32[]{:S(2)}) async-start(), calls=%async_computation.6 | async-start | bytes 7864320 | tf_op jit(solution)/shard_map/all_gather | solution.py:264
  175.7 112.7 %copy-start.6 = (bf16[768,1024]{1,0:T(8,128)(2,1)}, bf16[768,1024]{1,0:T(8,128)(2,1)S(1)}, u32[]{:S(2)}) copy-start(bf16[768,1024]{1,0:T(8,128)(2,1)S(1)} %fusion.28) | copy-start | bytes 4718596
  221.5 458.2 %all-gather.24.cloned.1.call-start = ((), (), s32[]{:S(2)}) async-start(), calls=%async_computation.7 | async-start | bytes 7864320 | tf_op jit(solution)/shard_map/all_gather | solution.py:265
  295.3 756.1 %all-reduce.15.cloned.1.call-start = ((), (), s32[]{:S(2)}) async-start(), calls=%async_computation.10 | async-start | bytes 16777216 | tf_op jit(solution)/shard_map/psum | solution.py:20
  354.0 94.2 %copy-start.37 = (bf16[3,256,16,64]{1,3,2,0:T(8,128)(2,1)S(1)}, bf16[3,256,16,64]{1,3,2,0:T(8,128)(2,1)}, u32[]{:S(2)}) copy-start(bf16[3,256,16,64]{1,3,2,0:T(8,128)(2,1)} %copy.77) | copy-start | bytes 4718596
  397.7 290.7 %copy-start.69 = (f32[3,16,1024]{2,1,0:T(8,128)}, f32[3,16,1024]{2,1,0:T(8,128)S(1)}, u32[]{:S(2)}) copy-start(f32[3,16,1024]{2,1,0:T(8,128)S(1)} %convert_element_type.203) | copy-start | bytes 589828
  500.8 63.6 %copy-start.13 = (bf16[3,256,16,48]{1,3,2,0:T(8,128)(2,1)S(1)}, bf16[3,256,16,48]{1,3,2,0:T(8,128)(2,1)}, u32[]{:S(2)}) copy-start(bf16[3,256,16,48]{1,3,2,0:T(8,128)(2,1)} %copy-done.12) | copy-start | bytes 3538948
  500.8 63.6 %copy-start.32 = (bf16[3,256,16,8]{1,3,2,0:T(8,128)(2,1)S(1)}, bf16[3,256,16,8]{1,3,2,0:T(8,128)(2,1)}, u32[]{:S(2)}) copy-start(bf16[3,256,16,8]{1,3,2,0:T(8,128)(2,1)} %copy-done.31) | copy-start | bytes 589828
  500.8 63.6 %copy-start.34 = (bf16[3,256,16,8]{1,3,2,0:T(8,128)(2,1)S(1)}, bf16[3,256,16,8]{1,3,2,0:T(8,128)(2,1)}, u32[]{:S(2)}) copy-start(bf16[3,256,16,8]{1,3,2,0:T(8,128)(2,1)} %copy-done.33) | copy-start | bytes 589828
  586.4 102.0 %copy-start.63 = (pred[1024,256]{1,0:T(8,128)(4,1)S(1)}, pred[1024,256]{1,0:T(8,128)(4,1)}, u32[]{:S(2)}) copy-start(pred[1024,256]{1,0:T(8,128)(4,1)} %iota_compare_fusion) | copy-start | bytes 786436
  760.1 421.8 %all-reduce.13.cloned.1.call-start = ((), (), s32[]{:S(2)}) async-start(), calls=%async_computation.9 | async-start | bytes 16777216 | tf_op jit(solution)/shard_map/psum | solution.py:21
  1051.4 166.8 %all-gather.26.cloned.1.call-start = ((), (), s32[]{:S(2)}) async-start(), calls=%async_computation.8 | async-start | bytes 2359296 | tf_op jit(solution)/shard_map/all_gather | solution.py:326
  1124.4 60.2 %copy-start.92 = (f32[1024]{0:T(1024)S(1)}, f32[1024]{0:T(1024)}, u32[]{:S(2)}) copy-start(f32[1024]{0:T(1024)} %convert_element_type.191) | copy-start | bytes 12292
  1124.4 60.2 %copy-start.93 = (f32[1024]{0:T(1024)S(1)}, f32[1024]{0:T(1024)}, u32[]{:S(2)}) copy-start(f32[1024]{0:T(1024)} %slice_convert_fusion.2) | copy-start | bytes 12292
  (95 other events, 967.4 us)
Sparse Core Ops, SparseCore 0:
  9.9 92.5 all-gather.9
  105.0 27.8 all-gather.11
  134.8 55.0 all-gather.17
  192.3 23.5 all-gather.19
  217.3 114.8 all-gather.15
  333.5 114.6 all-gather.13
  449.8 114.6 all-gather.21
  566.0 113.7 all-gather.23
  760.2 291.0 all-reduce.14
  1055.2 126.6 all-reduce.12
  1184.7 28.4 all-gather.25
